TPU v7x, 256 devices: a whole 4x4x8 slice. The times are simulated.
256 devices in a mesh: gx: 8 (over z), gy: 4 (over y), gz: 8 (over x, core).
Axes of the slice: x: 4, y: 4, z: 8, core: 2. Of those that a mesh axis runs over, the one named last changes fastest.
Arguments:
- fine_state: float32 [512, 5, 32, 1024], P(('gx', 'gy', 'gz')), may hold values from -1.2 to 3.5, as said below
- coarse_state: float32 [2048, 5, 16, 256], P(('gx', 'gy', 'gz')), may hold values from -1.2 to 3.5, as said below
- neighbours: int32 [512, 6], P(('gx', 'gy', 'gz')), may hold values from -1 to 511, as said below
- coarse_sources: int32 [512, 6], P(('gx', 'gy', 'gz')), may hold values from -1 to 2047, as said below
- covering: int32 [2048], P(('gx', 'gy', 'gz')), may hold values from -1 to 511, as said below
Outputs:
- fine_next: float32 [512, 5, 32, 1024], P(('gx', 'gy', 'gz'))
- coarse_next: float32 [2048, 5, 16, 256], P(('gx', 'gy', 'gz'))
Inputs may be any that keep to these rules, and one draw needn't show every extreme that they name: `fine_state`: each cell is the conserved state of density 0.5 to 2, velocity components -0.6 to 0.6 and pressure 0.4 to 1.6. `coarse_state`: each cell is the conserved state of density 0.5 to 2, velocity components -0.6 to 0.6 and pressure 0.4 to 1.6. For each box face exactly one of neighbours and coarse_sources is not -1; every box or block named lies on a device with the same gx index as the box; the faces of one device's boxes name at most 1 boxes or blocks held by any one device, and exactly 1 on some device. `coarse_sources`: see neighbours. `covering`: every fine box is named by exactly one block; a block and the box it names lie on devices with the same gy and gz index; the blocks of one device name at most 1 boxes of any one device, and exactly 1 of some device.
All inputs are finite; a program needn't handle non-finite values.
Results may differ from a plain program's by a relative error of at most 0.00005.
Values sent between devices are 32-bit elements; how exact they have to be, the bound alone decides.
No kernel may reach another device: no remote copies, remote signals or barrier semaphores. Data moves between devices by JAX's collectives and lax.ppermute only.
A program may use at most 64 MiB of HBM per device.

v0:
```python
import functools

import jax
import jax.numpy as jnp
from jax import lax
from jax.experimental import pallas as pl
from jax.experimental.pallas import tpu as pltpu
from jax.sharding import PartitionSpec as P


adiabatic = 5.0 / 3.0
courant = 0.12
AXES = ("gx", "gy", "gz")
PLANE = ("gy", "gz")

EDGE = 32
HALF = 16
FLAT = EDGE * EDGE
SMALL = HALF * HALF
LANES = 128
COMPS = 5
SLOT_ROWS = COMPS * FLAT // LANES


def iota(shape, dim):
    return lax.broadcasted_iota(jnp.int32, shape, dim)


def roll(x, shift, axis):
    size = x.shape[axis]
    shift = shift % size
    return x if shift == 0 else pltpu.roll(x, shift, axis)


def quotient(x, n):
    return lax.shift_right_logical(x, n.bit_length() - 1) if n & (n - 1) == 0 else lax.div(x, n)


def remainder(x, n):
    return lax.bitwise_and(x, n - 1) if n & (n - 1) == 0 else lax.rem(x, n)


def face_source(fine_ref, coarse_ref, box, side, boxes, blocks, line_size):
    fine_id = fine_ref[box, side]
    coarse_id = coarse_ref[box, side]
    is_fine = fine_id >= 0
    device = jnp.where(is_fine, quotient(fine_id, boxes), quotient(coarse_id, blocks))
    row = jnp.where(
        is_fine,
        remainder(fine_id, boxes) * 6 + (side ^ 1),
        boxes * 6 + remainder(coarse_id, blocks) * 6 + (side ^ 1),
    )
    return remainder(device, line_size), row


def request_kernel(
    boxes, blocks, line_size, fine_ref, coarse_ref, covering_ref, out_ref, wants_ref
):
    peers = iota(out_ref.shape, 0)
    table = jnp.zeros(out_ref.shape, jnp.int32)
    for box in range(boxes):
        for side in range(6):
            peer, row = face_source(fine_ref, coarse_ref, box, side, boxes, blocks, line_size)
            table = jnp.where(peers == peer, row + 1, table)
    out_ref[...] = table
    column = jnp.where(
        iota(wants_ref.shape, 0) == lax.axis_index("gx"), iota(wants_ref.shape, 1), -1
    )
    wants = jnp.zeros(wants_ref.shape, jnp.int32)
    for i in range(blocks):
        box = covering_ref[i]
        owner = jnp.where(box >= 0, quotient(quotient(box, boxes), line_size), -2)
        wants = jnp.where(column == owner, remainder(box, boxes) + 1, wants)
    wants_ref[...] = wants


def lane_gather(x, index):
    return jnp.take_along_axis(x, index, axis=1)


def row_gather(x, index):
    return jnp.take_along_axis(x, index, axis=0)


def table_kernel(boxes, blocks, fine_ref, coarse_ref, out_ref):
    row = iota((8, LANES), 0)
    lane = iota((8, LANES), 1)
    quad = lane // 32
    inner = lane % 32

    def fine_box(box, _):
        base = box * 6
        for comp in range(COMPS):
            dst = slice(8 * comp, 8 * comp + 8)
            for side, first in ((0, 0), (1, EDGE - 1)):
                for r in range(8):
                    out_ref[base + side, 8 * comp + r : 8 * comp + r + 1, :] = fine_ref[
                        box, comp, first : first + 1, LANES * r : LANES * r + LANES
                    ]
            y_low = jnp.zeros((8, LANES), jnp.float32)
            y_high = y_low
            z_low = y_low
            z_high = y_low
            for q in range(4):
                for v in range(8):
                    cells = fine_ref[box, comp, 8 * q : 8 * q + 8, LANES * v : LANES * v + LANES]
                    if v == 0:
                        y_low = jnp.where(quad == q, roll(cells, 32 * q, 1), y_low)
                    if v == 7:
                        y_high = jnp.where(quad == q, roll(cells, 32 * q - 96, 1), y_high)
                    spot = inner == 8 * q + v
                    z_low = jnp.where(spot, roll(cells, 8 * q + v, 1), z_low)
                    z_high = jnp.where(spot, roll(cells, 8 * q + v - 31, 1), z_high)
            out_ref[base + 2, dst, :] = y_low
            out_ref[base + 3, dst, :] = y_high
            out_ref[base + 4, dst, :] = z_low
            out_ref[base + 5, dst, :] = z_high
        return 0

    lax.fori_loop(0, boxes, fine_box, 0)

    pick_x = 32 * (row % 4) + 16 * (quad // 2) + inner // 2
    pick_y = inner // 2
    pick_z = 32 * (inner % 4) + 16 * (quad // 2)
    rows_y = 4 * (quad % 2) + row // 2
    rows_z = 4 * ((inner // 8) % 2) + row // 2

    def coarse_block(block, _):
        base = boxes * 6 + block * 6
        for comp in range(COMPS):
            dst = slice(8 * comp, 8 * comp + 8)
            cells = [
                [
                    coarse_ref[block, comp, 8 * g : 8 * g + 8, LANES * h : LANES * h + LANES]
                    for h in range(2)
                ]
                for g in range(2)
            ]
            for side, first in ((0, 0), (1, HALF - 1)):
                parts = [
                    jnp.broadcast_to(cells[first // 8][h][first % 8 : first % 8 + 1], (8, LANES))
                    for h in range(2)
                ]
                out_ref[base + side, dst, :] = jnp.where(
                    row < 4, lane_gather(parts[0], pick_x), lane_gather(parts[1], pick_x)
                )
            for side, half, start in ((2, 0, 0), (3, 1, LANES - HALF)):
                parts = [
                    row_gather(lane_gather(cells[g][half], pick_y + start), rows_y)
                    for g in range(2)
                ]
                out_ref[base + side, dst, :] = jnp.where(quad < 2, parts[0], parts[1])
            for side, last in ((4, 0), (5, HALF - 1)):
                parts = [
                    row_gather(
                        jnp.where(
                            inner % 8 < 4,
                            lane_gather(cells[g][0], pick_z + last),
                            lane_gather(cells[g][1], pick_z + last),
                        ),
                        rows_z,
                    )
                    for g in range(2)
                ]
                out_ref[base + side, dst, :] = jnp.where(inner < 16, parts[0], parts[1])
        return 0

    lax.fori_loop(0, blocks, coarse_block, 0, unroll=2)


def primitives(cells):
    inverse = 1.0 / cells[0]
    kinetic = (
        0.5 * (cells[1] * cells[1] + cells[2] * cells[2] + cells[3] * cells[3]) * inverse
    )
    pressure = (adiabatic - 1.0) * (cells[4] - kinetic)
    sound = jnp.sqrt(adiabatic * pressure * inverse)
    return inverse, pressure, sound


def physical_flux(cells, normal, speed, pressure):
    entries = [
        cells[normal],
        cells[1] * speed,
        cells[2] * speed,
        cells[3] * speed,
        (cells[4] + pressure) * speed,
    ]
    entries[normal] = entries[normal] + pressure
    return entries


def face_flux(low, high, low_flux, high_flux, low_fast, high_fast):
    fastest = jnp.maximum(low_fast, high_fast)
    return [
        (low_flux[k] + high_flux[k]) - fastest * (high[k] - low[k]) for k in range(COMPS)
    ]


def add_steps(total, cells, normal, speed, pressure, fast, keep, step, axis):
    flux = physical_flux(cells, normal, speed, pressure)
    upper = face_flux(
        cells,
        [roll(c, -step, axis) for c in cells],
        flux,
        [roll(c, -step, axis) for c in flux],
        fast,
        roll(fast, -step, axis),
    )
    upper = [jnp.where(keep, c, 0.0) for c in upper]
    steps = [c - roll(c, step, axis) for c in upper]
    return steps if total is None else [total[k] + steps[k] for k in range(COMPS)]


def interior_kernel(
    boxes,
    fine_ref,
    wants_a,
    wants_b,
    partial_ref,
    restricted_ref,
    wants_ref,
    out_ref,
    coarse_ref,
    speed_ref,
    pressure_ref,
    fast_ref,
    pair_ref,
    sems,
):
    wants_ref[...] = wants_a[...] + wants_b[...]
    columns = FLAT // LANES
    row = iota((EDGE, LANES), 0)
    lane = iota((EDGE, LANES), 1)

    def column(step, _):
        box = step // columns
        at = pl.ds(pl.multiple_of((step % columns) * LANES, LANES), LANES)
        cells = [fine_ref[box, k, :, at] for k in range(COMPS)]
        inverse, pressure, sound = primitives(cells)
        speed_y = cells[2] * inverse
        there = pl.ds(pl.multiple_of(step * LANES, LANES), LANES)
        speed_ref[:, there] = speed_y
        pressure_ref[:, there] = pressure
        fast_ref[:, there] = jnp.abs(speed_y) + sound
        total = None
        for normal, axis, keep in ((1, 0, row < EDGE - 1), (3, 1, lane % EDGE < EDGE - 1)):
            speed = cells[normal] * inverse
            total = add_steps(
                total, cells, normal, speed, pressure, jnp.abs(speed) + sound, keep, 1, axis
            )
        for k in range(COMPS):
            out_ref[box, k, :, at] = total[k]
        return 0

    lax.fori_loop(0, boxes * columns, column, 0, unroll=2)
    wide = iota((8, FLAT), 1)

    def rows(step, _):
        box = step // 4
        at = pl.ds(pl.multiple_of((step % 4) * 8, 8), 8)
        along = pl.ds(pl.multiple_of(box * FLAT, FLAT), FLAT)
        cells = [fine_ref[box, k, at, :] for k in range(COMPS)]
        speed, pressure, fast = [ref[at, along] for ref in (speed_ref, pressure_ref, fast_ref)]
        total = [out_ref[box, k, at, :] for k in range(COMPS)]
        keep = wide < FLAT - EDGE
        total = add_steps(total, cells, 2, speed, pressure, fast, keep, EDGE, 1)
        for k in range(COMPS):
            out_ref[box, k, at, :] = cells[k] - (0.5 * courant) * total[k]
        return 0

    lax.fori_loop(0, boxes * 4, rows, 0)
    save = pltpu.make_async_copy(out_ref, partial_ref, sems.at[0])
    save.start()
    lane16 = iota((HALF, LANES), 1)
    pick = 64 * ((lane16 // HALF) % 2) + 2 * (lane16 % HALF)

    def restrict(step, _):
        box = step // COMPS
        comp = step % COMPS
        for h in range(2):
            total = jnp.zeros((HALF, LANES), jnp.float32)
            for w in range(4):
                v = 4 * h + w
                pair_ref[v] = out_ref[box, comp, :, LANES * v : LANES * v + LANES]
                pair = (
                    pair_ref[v, pl.ds(0, HALF, stride=2), :]
                    + pair_ref[v, pl.ds(1, HALF, stride=2), :]
                )
                pair = pair + roll(pair, -EDGE, 1)
                pair = pair + roll(pair, -1, 1)
                total = jnp.where(lane16 // 32 == w, lane_gather(pair, pick), total)
            coarse_ref[box, comp, :, LANES * h : LANES * h + LANES] = 0.125 * total
        return 0

    lax.fori_loop(0, boxes * COMPS, restrict, 0, unroll=2)
    last = pltpu.make_async_copy(coarse_ref, restricted_ref, sems.at[1])
    last.start()
    save.wait()
    last.wait()


def reply_kernel(code_ref, table_ref, wants_a, wants_b, out_ref, wants_ref, codes, sem, sems):
    slots = out_ref.shape[0]
    rows = table_ref.shape[0]
    copy = pltpu.make_async_copy(code_ref, codes, sem)
    copy.start()
    copy.wait()

    def each(act):
        for i in range(slots):
            code = codes[i, 0]

            @pl.when(code > 0)
            def _(i=i, code=code):
                source = table_ref.at[jnp.clip(code - 1, 0, rows - 1)]
                act(pltpu.make_async_copy(source, out_ref.at[i], sems.at[i]))

    each(lambda copy: copy.start())
    wants_ref[...] = wants_a[...] + wants_b[...]
    each(lambda copy: copy.wait())


def flux_kernel(
    boxes,
    blocks,
    line_size,
    fine_ids,
    coarse_ids,
    restricted_ref,
    table_ref,
    replies_ref,
    wants_a,
    wants_b,
    flux_ref,
    send_ref,
    interior_ref,
    coarse_ref,
    wants_ref,
    wanted,
    fetch_sems,
    sems,
):
    me = lax.axis_index("gx")
    wants_ref[...] = wants_a[...] + wants_b[...]
    fetches = [
        pltpu.make_async_copy(wants_ref, wanted, fetch_sems.at[0]),
        pltpu.make_async_copy(restricted_ref, interior_ref, fetch_sems.at[1]),
    ]
    for fetch in fetches:
        fetch.start()
    for face in range(6 * boxes):
        box, side = face // 6, face % 6
        normal = side // 2 + 1
        peer, _ = face_source(fine_ids, coarse_ids, box, side, boxes, blocks, line_size)
        own = [table_ref[face, 8 * k : 8 * k + 8, :] for k in range(COMPS)]
        ghost = [replies_ref[peer, 8 * k : 8 * k + 8, :] for k in range(COMPS)]
        sides = []
        for cells in (own, ghost):
            inverse, pressure, sound = primitives(cells)
            speed = cells[normal] * inverse
            flux = physical_flux(cells, normal, speed, pressure)
            sides.append((cells, flux, jnp.abs(speed) + sound))
        low, high = sides[::-1] if side % 2 == 0 else sides
        flux = face_flux(low[0], high[0], low[1], high[1], low[2], high[2])
        flux = [(0.5 * courant) * c for c in flux]
        for k in range(COMPS):
            flux_ref[face, 8 * k : 8 * k + 8, :] = flux[k]

    row = iota((8, LANES), 0)
    lane = iota((8, LANES), 1)
    even = 2 * (row % 4)

    def restrict(comp, box):
        at = slice(8 * comp, 8 * comp + 8)
        faces = [
            flux_ref[box * 6 + side, at, :] * (0.125 if side % 2 == 0 else -0.125)
            for side in range(6)
        ]
        for side in range(6):
            face = faces[side]
            if side < 2:
                face = face + roll(face, -1, 1)
                face = face + roll(face, -EDGE, 1)
                face = lane_gather(face, 64 * ((lane // HALF) % 2) + 2 * (lane % HALF))
            else:
                face = face + roll(face, -1, 0)
                face = face + roll(face, -1 if side < 4 else -EDGE, 1)
                face = row_gather(face, even)
            faces[side] = face
        for t in range(2):
            quarter = 2 * t + row // 4
            for h in range(2):
                spot = (box, comp, slice(8 * t, 8 * t + 8), slice(LANES * h, LANES * h + LANES))
                cells = interior_ref[spot]
                pick = 64 * ((lane // HALF) % 2) + 8 * quarter + 4 * h + lane // 32
                cells = cells + jnp.where(lane % HALF == 0, lane_gather(faces[4], pick), 0.0)
                cells = cells + jnp.where(
                    lane % HALF == HALF - 1, lane_gather(faces[5], pick), 0.0
                )
                pick = 32 * quarter + 2 * (lane % HALF)
                near_edge = lane < HALF if h == 0 else lane >= LANES - HALF
                cells = cells + jnp.where(near_edge, lane_gather(faces[2 + h], pick), 0.0)
                first = row == 0 if t == 0 else row == 7
                cells = cells + jnp.where(first, row_gather(faces[t], 4 * h + lane // 32), 0.0)
                coarse_ref[spot] = cells

    def each(box, act):
        for i in range(send_ref.shape[0]):

            @pl.when(wanted[i, me] == box + 1)
            def _(i=i):
                act(pltpu.make_async_copy(coarse_ref.at[box], send_ref.at[i], sems.at[i]))

    for fetch in fetches:
        fetch.wait()
    for box in range(boxes):
        for comp in range(COMPS):
            restrict(comp, box)
        each(box, lambda copy: copy.start())
    for box in range(boxes):
        each(box, lambda copy: copy.wait())


def finish_kernel(boxes, partial_ref, flux_ref, out_ref):
    row = iota((8, LANES), 0)
    lane = iota((8, LANES), 1)
    inner = lane % 32

    def plane(step, _):
        box = step // COMPS
        comp = step % COMPS
        at = pl.ds(pl.multiple_of(comp * 8, 8), 8)
        faces = [flux_ref[box * 6 + side, at, :] for side in range(6)]
        for q in range(4):
            for v in range(8):
                spot = (box, comp, slice(8 * q, 8 * q + 8), slice(LANES * v, LANES * v + LANES))
                cells = partial_ref[spot]
                shift = 8 * q + v
                cells = cells + jnp.where(inner == 0, roll(faces[4], -shift, 1), 0.0)
                cells = cells - jnp.where(inner == 31, roll(faces[5], 31 - shift, 1), 0.0)
                if v == 0:
                    cells = cells + jnp.where(lane < 32, roll(faces[2], -32 * q, 1), 0.0)
                if v == 7:
                    cells = cells - jnp.where(lane >= 96, roll(faces[3], 96 - 32 * q, 1), 0.0)
                if q == 0:
                    cells = cells + jnp.where(row == 0, faces[0][v : v + 1], 0.0)
                if q == 3:
                    cells = cells - jnp.where(row == 7, faces[1][v : v + 1], 0.0)
                out_ref[spot] = cells
        return 0

    lax.fori_loop(0, boxes * COMPS, plane, 0)


def copy_kernel(x_ref, out_ref):
    out_ref[...] = x_ref[...]


def place_kernel(boxes, line_size, covering_ref, _, source_ref, out_ref, sems):
    def each(act):
        for i in range(out_ref.shape[0]):
            box = covering_ref[i]

            @pl.when(box >= 0)
            def _(i=i, box=box):
                column = quotient(quotient(box, boxes), line_size)
                column = jnp.clip(column, 0, source_ref.shape[0] - 1)
                act(pltpu.make_async_copy(source_ref.at[column], out_ref.at[i], sems.at[i]))

    each(lambda copy: copy.start())
    each(lambda copy: copy.wait())


def any_spec():
    return pl.BlockSpec(memory_space=pl.ANY)


def hbm_spec():
    return pl.BlockSpec(memory_space=pltpu.HBM)


def smem_spec():
    return pl.BlockSpec(memory_space=pltpu.SMEM)


def vmem_spec():
    return pl.BlockSpec(memory_space=pltpu.VMEM)


def kernel_params(mib=16):
    return pltpu.CompilerParams(vmem_limit_bytes=mib << 20)


def near(x):
    return pltpu.with_memory_space_constraint(x, pltpu.VMEM)


def far(x):
    return pltpu.with_memory_space_constraint(x, pltpu.HBM)


def exchange(x):
    return lax.all_to_all(x, PLANE, split_axis=0, concat_axis=0, tiled=True)


def body(fine_state, coarse_state, neighbours, coarse_sources, covering):
    boxes = fine_state.shape[0]
    blocks = coarse_state.shape[0]
    line_size = lax.axis_size("gy") * lax.axis_size("gz")
    ring = lax.axis_size("gx")
    f32 = jnp.float32

    tile = (ring, LANES)

    def across(x, bit):
        return lax.ppermute(x, "gx", [(i, i ^ bit) for i in range(ring)])

    requests, wants = pl.pallas_call(
        functools.partial(request_kernel, boxes, blocks, line_size),
        out_shape=(
            jax.ShapeDtypeStruct((line_size, LANES), jnp.int32),
            pltpu.VMEM(tile, jnp.int32),
        ),
        in_specs=[smem_spec()] * 3,
        out_specs=(vmem_spec(), vmem_spec()),
        name="requests",
    )(far(neighbours), far(coarse_sources), far(covering))
    other = across(wants, 4)
    codes = exchange(requests)

    table = pl.pallas_call(
        functools.partial(table_kernel, boxes, blocks),
        out_shape=pltpu.VMEM((6 * (boxes + blocks), SLOT_ROWS, LANES), f32),
        in_specs=[vmem_spec(), vmem_spec()],
        out_specs=vmem_spec(),
        name="tables",
    )(fine_state, coarse_state)

    answers, wants = pl.pallas_call(
        reply_kernel,
        out_shape=(
            pltpu.HBM((line_size, SLOT_ROWS, LANES), f32),
            pltpu.VMEM(tile, jnp.int32),
        ),
        in_specs=[vmem_spec()] * 4,
        out_specs=(hbm_spec(), vmem_spec()),
        scratch_shapes=[
            pltpu.SMEM((line_size, LANES), jnp.int32),
            pltpu.SemaphoreType.DMA,
            pltpu.SemaphoreType.DMA((line_size,)),
        ],
        compiler_params=kernel_params(),
        name="answers",
    )(near(codes), near(table), near(wants), near(other))
    other = across(wants, 1)
    replies = exchange(answers)

    partial, interior, wants = pl.pallas_call(
        functools.partial(interior_kernel, boxes),
        out_shape=(
            pltpu.HBM(fine_state.shape, f32),
            pltpu.HBM((boxes, COMPS, HALF, SMALL), f32),
            pltpu.VMEM(tile, jnp.int32),
        ),
        in_specs=[vmem_spec()] * 3,
        out_specs=(hbm_spec(), hbm_spec(), vmem_spec()),
        scratch_shapes=[
            pltpu.VMEM(fine_state.shape, f32),
            pltpu.VMEM((boxes, COMPS, HALF, SMALL), f32),
        ]
        + [pltpu.VMEM((EDGE, boxes * FLAT), f32)] * 3
        + [pltpu.VMEM((8, EDGE, LANES), f32), pltpu.SemaphoreType.DMA((2,))],
        compiler_params=kernel_params(),
        name="interior",
    )(fine_state, near(wants), near(other))
    other = across(wants, 2)


    flux, sent = pl.pallas_call(
        functools.partial(flux_kernel, boxes, blocks, line_size),
        out_shape=(
            pltpu.VMEM((6 * boxes, SLOT_ROWS, LANES), f32),
            pltpu.HBM((ring, COMPS, HALF, SMALL), f32),
        ),
        in_specs=[smem_spec()] * 2 + [hbm_spec()] + [vmem_spec()] * 4,
        out_specs=(vmem_spec(), hbm_spec()),
        scratch_shapes=[
            pltpu.VMEM((boxes, COMPS, HALF, SMALL), f32),
            pltpu.VMEM((boxes, COMPS, HALF, SMALL), f32),
            pltpu.VMEM(tile, jnp.int32),
            pltpu.SMEM(tile, jnp.int32),
            pltpu.SemaphoreType.DMA((2,)),
            pltpu.SemaphoreType.DMA((ring,)),
        ],
        compiler_params=kernel_params(),
        name="fluxes",
    )(
        far(neighbours),
        far(coarse_sources),
        far(interior),
        near(table),
        near(replies),
        near(wants),
        near(other),
    )
    received = lax.all_to_all(sent, "gx", split_axis=0, concat_axis=0, tiled=True)

    fine_next = pl.pallas_call(
        functools.partial(finish_kernel, boxes),
        out_shape=jax.ShapeDtypeStruct(fine_state.shape, f32),
        in_specs=[vmem_spec(), vmem_spec()],
        out_specs=vmem_spec(),
        compiler_params=kernel_params(),
        name="finish",
    )(partial, near(flux))

    prior = pl.pallas_call(
        copy_kernel,
        out_shape=jax.ShapeDtypeStruct(coarse_state.shape, f32),
        in_specs=[vmem_spec()],
        out_specs=vmem_spec(),
        compiler_params=kernel_params(),
        name="prior",
    )(coarse_state)

    coarse_next = pl.pallas_call(
        functools.partial(place_kernel, boxes, line_size),
        out_shape=jax.ShapeDtypeStruct(coarse_state.shape, f32),
        in_specs=[smem_spec(), any_spec(), vmem_spec()],
        out_specs=any_spec(),
        scratch_shapes=[pltpu.SemaphoreType.DMA((blocks,))],
        input_output_aliases={1: 0},
        compiler_params=kernel_params(),
        name="place",
    )(far(covering), prior, near(received))
    return fine_next, coarse_next


def solution(mesh):
    spec = P(AXES)
    return jax.shard_map(
        body, mesh=mesh, in_specs=(spec,) * 5, out_specs=(spec, spec), check_vma=False
    )
```

profile of v0, /device:TPU:1, one launch (start us, length us, event | category | flops | bytes accessed | tf_op | source)
XLA Modules:
  0.0 73.2 jit_solution(6629055652171861230)
XLA Ops:
  0.6 1.4 %requests.1 = (s32[32,128]{1,0:T(8,128)}, s32[8,128]{1,0:T(8,128)S(1)}) custom-call(s32[2,6]{1,0:T(2,128)} %fine_ids.1, s32[2,6]{1,0:T(2,128)} %coarse_ids.1, s32[8]{0:T(128)} %covering_ref.3), custom_call_target="tpu_custom_call" | custom-call | tf_op jit(solution)/shard_map/requests/pallas_call | solution.py:519
  2.0 8.6 %all-to-all-start = ((s32[32,1,128]{2,1,0:T(1,128)}), s32[32,1,128]{2,1,0:T(1,128)S(1)}, u32[]{:S(2)}, u32[]{:S(2)}) async-start(s32[32,1,128]{2,1,0:T(1,128)} %bitcast.5), calls=%async_computation | async-start | bytes 32768 | tf_op jit(solution)/shard_map/all_to_all | solution.py:504
  10.6 7.0 %collective-permute-start = (s32[8,128]{1,0:T(8,128)S(1)}, s32[8,128]{1,0:T(8,128)S(1)}, u32[]{:S(2)}, u32[]{:S(2)}) collective-permute-start(s32[8,128]{1,0:T(8,128)S(1)} %get-tuple-element.12.wants_a), channel_id=1, source_target_pairs={{0,128},{32,160},{64,192},{96,224},{128,0},{160,32},{192,64},{224,... | collective-permute-start | bytes 12296 | tf_op jit(solution)/shard_map/ppermute | solution.py:517
  17.6 3.9 %tables.1.table_ref = f32[60,40,128]{2,1,0:T(8,128)S(1)} custom-call(f32[2,5,32,1024]{3,2,1,0:T(8,128)} %fine_ref.5, f32[8,5,16,256]{3,2,1,0:T(8,128)} %x_ref.1), custom_call_target="tpu_custom_call" | custom-call | tf_op jit(solution)/shard_map/tables/pallas_call | solution.py:532
  21.5 0.0 copy-start
  21.5 0.0 collective-permute-done.wants_b
  21.5 0.0 all-to-all-done
  21.5 1.8 %answers.1 = (f32[32,40,128]{2,1,0:T(8,128)}, s32[8,128]{1,0:T(8,128)S(1)}) custom-call(s32[32,128]{1,0:T(8,128)S(1)} %bitcast.4, f32[60,40,128]{2,1,0:T(8,128)S(1)} %tables.1.table_ref, s32[8,128]{1,0:T(8,128)S(1)} %get-tuple-element.12.wants_a, s32[8,128]{1,0:T(8,128)S(1)} %collective-permute-done.wants_b), custom_call_target="tpu_custom_call" | custom-call | tf_op jit(solution)/shard_map/answers/pallas_call | solution.py:540
  23.3 7.7 %all-to-all-start.1 = ((f32[32,40,128]{2,1,0:T(8,128)}), f32[32,40,128]{2,1,0:T(8,128)S(1)}, u32[]{:S(2)}, u32[]{:S(2)}) async-start(f32[32,40,128]{2,1,0:T(8,128)} %get-tuple-element.16), calls=%async_computation.1 | async-start | bytes 1310720 | tf_op jit(solution)/shard_map/all_to_all | solution.py:504
  31.0 0.8 %collective-permute-start.1 = (s32[8,128]{1,0:T(8,128)S(1)}, s32[8,128]{1,0:T(8,128)S(1)}, u32[]{:S(2)}, u32[]{:S(2)}) collective-permute-start(s32[8,128]{1,0:T(8,128)S(1)} %get-tuple-element.13.wants_a), channel_id=1, source_target_pairs={{0,32},{32,0},{64,96},{96,64},{128,160},{160,128},{192,224},{224,1... | collective-permute-start | bytes 12296 | tf_op jit(solution)/shard_map/ppermute | solution.py:517
  31.8 2.0 %collective-permute-done.1.wants_b = s32[8,128]{1,0:T(8,128)S(1)} collective-permute-done((s32[8,128]{1,0:T(8,128)S(1)}, s32[8,128]{1,0:T(8,128)S(1)}, u32[]{:S(2)}, u32[]{:S(2)}) %collective-permute-start.1) | collective-permute-done | bytes 4128 | tf_op jit(solution)/shard_map/ppermute | solution.py:517
  33.8 0.0 copy-done
  33.8 5.9 %interior.1 = (f32[2,5,32,1024]{3,2,1,0:T(8,128)}, f32[2,5,16,256]{3,2,1,0:T(8,128)}, s32[8,128]{1,0:T(8,128)S(1)}) custom-call(f32[2,5,32,1024]{3,2,1,0:T(8,128)S(1)} %copy-done, s32[8,128]{1,0:T(8,128)S(1)} %get-tuple-element.13.wants_a, s32[8,128]{1,0:T(8,128)S(1)} %collective-permute-done.1.wants_b), custom_call_target="tpu_custom_call" | custom-call | tf_op jit(solution)/shard_map/interior/pallas_call | solution.py:559
  39.7 1.3 %collective-permute-start.2 = (s32[8,128]{1,0:T(8,128)S(1)}, s32[8,128]{1,0:T(8,128)S(1)}, u32[]{:S(2)}, u32[]{:S(2)}) collective-permute-start(s32[8,128]{1,0:T(8,128)S(1)} %get-tuple-element.17.wants_a), channel_id=1, source_target_pairs={{0,64},{32,96},{64,0},{96,32},{128,192},{160,224},{192,128},{224,1... | collective-permute-start | bytes 12296 | tf_op jit(solution)/shard_map/ppermute | solution.py:517
  41.0 2.5 %collective-permute-done.2.wants_b = s32[8,128]{1,0:T(8,128)S(1)} collective-permute-done((s32[8,128]{1,0:T(8,128)S(1)}, s32[8,128]{1,0:T(8,128)S(1)}, u32[]{:S(2)}, u32[]{:S(2)}) %collective-permute-start.2) | collective-permute-done | bytes 4128 | tf_op jit(solution)/shard_map/ppermute | solution.py:517
  43.4 0.4 all-to-all-done.1.replies_ref
  43.8 0.0 copy-start.1
  43.8 3.9 %fluxes.1 = (f32[12,40,128]{2,1,0:T(8,128)S(1)}, f32[8,5,16,256]{3,2,1,0:T(8,128)}) custom-call(s32[2,6]{1,0:T(2,128)} %fine_ids.1, s32[2,6]{1,0:T(2,128)} %coarse_ids.1, f32[2,5,16,256]{3,2,1,0:T(8,128)} %get-tuple-element.15.restricted_ref, f32[60,40,128]{2,1,0:T(8,128)S(1)} %tables.1.table_ref, f32[32,40,128]{2,1,0:T(8,128)S(1)} %all-to-all-done.1.replies_ref, ...), custom_call_target="tpu_custom_call" | custom-call | tf_op jit(solution)/shard_map/fluxes/pallas_call | solution.py:580
  47.8 0.0 copy-start.2
  47.8 4.7 %all-to-all-start.2 = ((f32[8,5,16,256]{3,2,1,0:T(8,128)}), f32[8,5,16,256]{3,2,1,0:T(8,128)S(1)}, u32[]{:S(2)}, u32[]{:S(2)}) async-start(f32[8,5,16,256]{3,2,1,0:T(8,128)} %get-tuple-element.19), calls=%async_computation.2 | async-start | bytes 1310720 | tf_op jit(solution)/shard_map/all_to_all | solution.py:607
  52.5 0.0 copy-done.1
  52.5 0.9 %prior.1._ = f32[8,5,16,256]{3,2,1,0:T(8,128)} custom-call(f32[8,5,16,256]{3,2,1,0:T(8,128)S(1)} %copy-done.1), custom_call_target="tpu_custom_call" | custom-call | tf_op jit(solution)/shard_map/prior/pallas_call | solution.py:618
  53.4 0.0 copy-done.2
  53.4 2.5 %finish.1 = f32[2,5,32,1024]{3,2,1,0:T(8,128)} custom-call(f32[2,5,32,1024]{3,2,1,0:T(8,128)S(1)} %copy-done.2, f32[12,40,128]{2,1,0:T(8,128)S(1)} %get-tuple-element.18.flux_ref), custom_call_target="tpu_custom_call" | custom-call | tf_op jit(solution)/shard_map/finish/pallas_call | solution.py:609
  55.9 15.8 %all-to-all-done.2.source_ref = f32[8,5,16,256]{3,2,1,0:T(8,128)S(1)} async-done(((f32[8,5,16,256]{3,2,1,0:T(8,128)}), f32[8,5,16,256]{3,2,1,0:T(8,128)S(1)}, u32[]{:S(2)}, u32[]{:S(2)}) %all-to-all-start.2) | async-done | bytes 655392 | tf_op jit(solution)/shard_map/all_to_all | solution.py:607
  71.7 1.5 %place.1 = f32[8,5,16,256]{3,2,1,0:T(8,128)} custom-call(s32[8]{0:T(128)} %covering_ref.3, f32[8,5,16,256]{3,2,1,0:T(8,128)} %prior.1._, f32[8,5,16,256]{3,2,1,0:T(8,128)S(1)} %all-to-all-done.2.source_ref), custom_call_target="tpu_custom_call", output_to_operand_aliasing={{}: (1, {})} | custom-call | tf_op jit(solution)/shard_map/place/pallas_call | solution.py:627
Async XLA Ops:
  2.0 19.5 %all-to-all-start = ((s32[32,1,128]{2,1,0:T(1,128)}), s32[32,1,128]{2,1,0:T(1,128)S(1)}, u32[]{:S(2)}, u32[]{:S(2)}) async-start(s32[32,1,128]{2,1,0:T(1,128)} %bitcast.5), calls=%async_computation | async-start | bytes 32768 | tf_op jit(solution)/shard_map/all_to_all | solution.py:504
  10.6 10.9 %collective-permute-start = (s32[8,128]{1,0:T(8,128)S(1)}, s32[8,128]{1,0:T(8,128)S(1)}, u32[]{:S(2)}, u32[]{:S(2)}) collective-permute-start(s32[8,128]{1,0:T(8,128)S(1)} %get-tuple-element.12.wants_a), channel_id=1, source_target_pairs={{0,128},{32,160},{64,192},{96,224},{128,0},{160,32},{192,64},{224,... | collective-permute-start | bytes 12296 | tf_op jit(solution)/shard_map/ppermute | solution.py:517
  21.5 12.4 %copy-start = (f32[2,5,32,1024]{3,2,1,0:T(8,128)S(1)}, f32[2,5,32,1024]{3,2,1,0:T(8,128)}, u32[]{:S(2)}) copy-start(f32[2,5,32,1024]{3,2,1,0:T(8,128)} %fine_ref.5) | copy-start | bytes 3932164
  23.3 20.5 %all-to-all-start.1 = ((f32[32,40,128]{2,1,0:T(8,128)}), f32[32,40,128]{2,1,0:T(8,128)S(1)}, u32[]{:S(2)}, u32[]{:S(2)}) async-start(f32[32,40,128]{2,1,0:T(8,128)} %get-tuple-element.16), calls=%async_computation.1 | async-start | bytes 1310720 | tf_op jit(solution)/shard_map/all_to_all | solution.py:504
  31.0 2.8 %collective-permute-start.1 = (s32[8,128]{1,0:T(8,128)S(1)}, s32[8,128]{1,0:T(8,128)S(1)}, u32[]{:S(2)}, u32[]{:S(2)}) collective-permute-start(s32[8,128]{1,0:T(8,128)S(1)} %get-tuple-element.13.wants_a), channel_id=1, source_target_pairs={{0,32},{32,0},{64,96},{96,64},{128,160},{160,128},{192,224},{224,1... | collective-permute-start | bytes 12296 | tf_op jit(solution)/shard_map/ppermute | solution.py:517
  39.7 3.7 %collective-permute-start.2 = (s32[8,128]{1,0:T(8,128)S(1)}, s32[8,128]{1,0:T(8,128)S(1)}, u32[]{:S(2)}, u32[]{:S(2)}) collective-permute-start(s32[8,128]{1,0:T(8,128)S(1)} %get-tuple-element.17.wants_a), channel_id=1, source_target_pairs={{0,64},{32,96},{64,0},{96,32},{128,192},{160,224},{192,128},{224,1... | collective-permute-start | bytes 12296 | tf_op jit(solution)/shard_map/ppermute | solution.py:517
  43.8 8.7 %copy-start.1 = (f32[8,5,16,256]{3,2,1,0:T(8,128)S(1)}, f32[8,5,16,256]{3,2,1,0:T(8,128)}, u32[]{:S(2)}) copy-start(f32[8,5,16,256]{3,2,1,0:T(8,128)} %x_ref.1) | copy-start | bytes 1966084
  47.8 5.6 %copy-start.2 = (f32[2,5,32,1024]{3,2,1,0:T(8,128)S(1)}, f32[2,5,32,1024]{3,2,1,0:T(8,128)}, u32[]{:S(2)}) copy-start(f32[2,5,32,1024]{3,2,1,0:T(8,128)} %get-tuple-element.14.partial_ref) | copy-start | bytes 3932164
  47.8 23.9 %all-to-all-start.2 = ((f32[8,5,16,256]{3,2,1,0:T(8,128)}), f32[8,5,16,256]{3,2,1,0:T(8,128)S(1)}, u32[]{:S(2)}, u32[]{:S(2)}) async-start(f32[8,5,16,256]{3,2,1,0:T(8,128)} %get-tuple-element.19), calls=%async_computation.2 | async-start | bytes 1310720 | tf_op jit(solution)/shard_map/all_to_all | solution.py:607
where the time goes:
time: 73.6 us; the launch traced here: 73.2 us
  starting transfers between devices  30.1 us (41%)
  Pallas kernels  21.7 us (29%)
  waiting for transfers between devices  20.7 us (28%)
    all_to_all x2, starting transfers between devices, exchange(): return lax.all_to_all(x, PLANE, split_axis=0, concat_axis=0, tiled=True)  16.2 us
    all_to_all x1, waiting for transfers between devices, body(): lax.all_to_all(sent, 'gx', split_axis=0, concat_axis=0, tiled=True)  15.8 us
    ppermute x3, starting transfers between devices, across(): return lax.ppermute(x, 'gx', [(i, i ^ bit) for i in range(ring)])  9.1 us
    pallas_call x1, Pallas kernels, body(): pl.pallas_call(functools.partial(interior_kernel, boxes), out_shape=(pltp...  5.85 us
    all_to_all x1, starting transfers between devices, body(): lax.all_to_all(sent, 'gx', split_axis=0, concat_axis=0, tiled=True)  4.74 us
    ppermute x3, waiting for transfers between devices, across(): return lax.ppermute(x, 'gx', [(i, i ^ bit) for i in range(ring)])  4.47 us
    pallas_call x1, Pallas kernels, body(): pl.pallas_call(functools.partial(flux_kernel, boxes, blocks, line_size),...  3.91 us
    pallas_call x1, Pallas kernels, body(): pl.pallas_call(functools.partial(table_kernel, boxes, blocks), out_shape=...  3.87 us
  transfers between devices with their start and end apart: 6, of which 4 were waited for; matrix products, arithmetic and copies ran while one was open for 0% of the time, Pallas kernels for 18%

commit v1 on v0

--- a/solution.py
+++ b/solution.py
@@ -53,9 +53,7 @@
     return remainder(device, line_size), row
 
 
-def request_kernel(
-    boxes, blocks, line_size, fine_ref, coarse_ref, covering_ref, out_ref, wants_ref
-):
+def request_kernel(boxes, blocks, line_size, fine_ref, coarse_ref, out_ref):
     peers = iota(out_ref.shape, 0)
     table = jnp.zeros(out_ref.shape, jnp.int32)
     for box in range(boxes):
@@ -63,15 +61,6 @@
             peer, row = face_source(fine_ref, coarse_ref, box, side, boxes, blocks, line_size)
             table = jnp.where(peers == peer, row + 1, table)
     out_ref[...] = table
-    column = jnp.where(
-        iota(wants_ref.shape, 0) == lax.axis_index("gx"), iota(wants_ref.shape, 1), -1
-    )
-    wants = jnp.zeros(wants_ref.shape, jnp.int32)
-    for i in range(blocks):
-        box = covering_ref[i]
-        owner = jnp.where(box >= 0, quotient(quotient(box, boxes), line_size), -2)
-        wants = jnp.where(column == owner, remainder(box, boxes) + 1, wants)
-    wants_ref[...] = wants
 
 
 def lane_gather(x, index):
@@ -215,11 +204,8 @@
 def interior_kernel(
     boxes,
     fine_ref,
-    wants_a,
-    wants_b,
     partial_ref,
     restricted_ref,
-    wants_ref,
     out_ref,
     coarse_ref,
     speed_ref,
@@ -228,7 +214,6 @@
     pair_ref,
     sems,
 ):
-    wants_ref[...] = wants_a[...] + wants_b[...]
     columns = FLAT // LANES
     row = iota((EDGE, LANES), 0)
     lane = iota((EDGE, LANES), 1)
@@ -300,7 +285,7 @@
     last.wait()
 
 
-def reply_kernel(code_ref, table_ref, wants_a, wants_b, out_ref, wants_ref, codes, sem, sems):
+def reply_kernel(code_ref, table_ref, out_ref, codes, sem, sems):
     slots = out_ref.shape[0]
     rows = table_ref.shape[0]
     copy = pltpu.make_async_copy(code_ref, codes, sem)
@@ -317,7 +302,6 @@
                 act(pltpu.make_async_copy(source, out_ref.at[i], sems.at[i]))
 
     each(lambda copy: copy.start())
-    wants_ref[...] = wants_a[...] + wants_b[...]
     each(lambda copy: copy.wait())
 
 
@@ -330,25 +314,12 @@
     restricted_ref,
     table_ref,
     replies_ref,
-    wants_a,
-    wants_b,
     flux_ref,
-    send_ref,
-    interior_ref,
-    coarse_ref,
-    wants_ref,
-    wanted,
-    fetch_sems,
-    sems,
+    *rest,
 ):
-    me = lax.axis_index("gx")
-    wants_ref[...] = wants_a[...] + wants_b[...]
-    fetches = [
-        pltpu.make_async_copy(wants_ref, wanted, fetch_sems.at[0]),
-        pltpu.make_async_copy(restricted_ref, interior_ref, fetch_sems.at[1]),
-    ]
-    for fetch in fetches:
-        fetch.start()
+    coarse_refs, (interior_ref, sem) = rest[:boxes], rest[boxes:]
+    fetch = pltpu.make_async_copy(restricted_ref, interior_ref, sem)
+    fetch.start()
     for face in range(6 * boxes):
         box, side = face // 6, face % 6
         normal = side // 2 + 1
@@ -391,8 +362,8 @@
         for t in range(2):
             quarter = 2 * t + row // 4
             for h in range(2):
-                spot = (box, comp, slice(8 * t, 8 * t + 8), slice(LANES * h, LANES * h + LANES))
-                cells = interior_ref[spot]
+                spot = (comp, slice(8 * t, 8 * t + 8), slice(LANES * h, LANES * h + LANES))
+                cells = interior_ref[(box,) + spot]
                 pick = 64 * ((lane // HALF) % 2) + 8 * quarter + 4 * h + lane // 32
                 cells = cells + jnp.where(lane % HALF == 0, lane_gather(faces[4], pick), 0.0)
                 cells = cells + jnp.where(
@@ -403,33 +374,20 @@
                 cells = cells + jnp.where(near_edge, lane_gather(faces[2 + h], pick), 0.0)
                 first = row == 0 if t == 0 else row == 7
                 cells = cells + jnp.where(first, row_gather(faces[t], 4 * h + lane // 32), 0.0)
-                coarse_ref[spot] = cells
-
-    def each(box, act):
-        for i in range(send_ref.shape[0]):
-
-            @pl.when(wanted[i, me] == box + 1)
-            def _(i=i):
-                act(pltpu.make_async_copy(coarse_ref.at[box], send_ref.at[i], sems.at[i]))
-
-    for fetch in fetches:
-        fetch.wait()
+                coarse_refs[box][spot] = cells
+
+    fetch.wait()
     for box in range(boxes):
         for comp in range(COMPS):
             restrict(comp, box)
-        each(box, lambda copy: copy.start())
-    for box in range(boxes):
-        each(box, lambda copy: copy.wait())
-
-
-def finish_kernel(boxes, partial_ref, flux_ref, out_ref):
+
+
+def finish_kernel(boxes, partial_ref, flux_ref, out_ref, next_ref, sems):
     row = iota((8, LANES), 0)
     lane = iota((8, LANES), 1)
     inner = lane % 32
 
-    def plane(step, _):
-        box = step // COMPS
-        comp = step % COMPS
+    def plane(comp, _, box):
         at = pl.ds(pl.multiple_of(comp * 8, 8), 8)
         faces = [flux_ref[box * 6 + side, at, :] for side in range(6)]
         for q in range(4):
@@ -447,29 +405,45 @@
                     cells = cells + jnp.where(row == 0, faces[0][v : v + 1], 0.0)
                 if q == 3:
                     cells = cells - jnp.where(row == 7, faces[1][v : v + 1], 0.0)
-                out_ref[spot] = cells
+                next_ref[spot] = cells
         return 0
 
-    lax.fori_loop(0, boxes * COMPS, plane, 0)
+    copies = []
+    for box in range(boxes):
+        lax.fori_loop(0, COMPS, functools.partial(plane, box=box), 0)
+        copy = pltpu.make_async_copy(next_ref.at[box], out_ref.at[box], sems.at[box])
+        copy.start()
+        copies.append(copy)
+    for copy in copies:
+        copy.wait()
 
 
 def copy_kernel(x_ref, out_ref):
     out_ref[...] = x_ref[...]
 
 
-def place_kernel(boxes, line_size, covering_ref, _, source_ref, out_ref, sems):
-    def each(act):
-        for i in range(out_ref.shape[0]):
-            box = covering_ref[i]
-
-            @pl.when(box >= 0)
-            def _(i=i, box=box):
-                column = quotient(quotient(box, boxes), line_size)
-                column = jnp.clip(column, 0, source_ref.shape[0] - 1)
-                act(pltpu.make_async_copy(source_ref.at[column], out_ref.at[i], sems.at[i]))
-
-    each(lambda copy: copy.start())
-    each(lambda copy: copy.wait())
+def place_kernel(boxes, line_size, ring, covering_ref, _, *rest):
+    sources = rest[: boxes * ring]
+    out_ref, sems = rest[boxes * ring], rest[boxes * ring + 1]
+    me = lax.axis_index("gx")
+    blocks = out_ref.shape[0]
+
+    for i in range(blocks):
+        box = covering_ref[i]
+        column = quotient(quotient(box, boxes), line_size)
+        away = remainder(column - me + ring, ring)
+        which = jnp.where(box >= 0, away * boxes + remainder(box, boxes), -1)
+        for k in range(boxes * ring):
+
+            @pl.when(which == k)
+            def _(i=i, k=k):
+                pltpu.make_async_copy(sources[k], out_ref.at[i], sems.at[i]).start()
+
+    for i in range(blocks):
+
+        @pl.when(covering_ref[i] >= 0)
+        def _(i=i):
+            pltpu.make_async_copy(sources[0], out_ref.at[i], sems.at[i]).wait()
 
 
 def any_spec():
@@ -511,22 +485,13 @@
     ring = lax.axis_size("gx")
     f32 = jnp.float32
 
-    tile = (ring, LANES)
-
-    def across(x, bit):
-        return lax.ppermute(x, "gx", [(i, i ^ bit) for i in range(ring)])
-
-    requests, wants = pl.pallas_call(
+    requests = pl.pallas_call(
         functools.partial(request_kernel, boxes, blocks, line_size),
-        out_shape=(
-            jax.ShapeDtypeStruct((line_size, LANES), jnp.int32),
-            pltpu.VMEM(tile, jnp.int32),
-        ),
-        in_specs=[smem_spec()] * 3,
-        out_specs=(vmem_spec(), vmem_spec()),
+        out_shape=jax.ShapeDtypeStruct((line_size, LANES), jnp.int32),
+        in_specs=[smem_spec(), smem_spec()],
+        out_specs=vmem_spec(),
         name="requests",
-    )(far(neighbours), far(coarse_sources), far(covering))
-    other = across(wants, 4)
+    )(far(neighbours), far(coarse_sources))
     codes = exchange(requests)
 
     table = pl.pallas_call(
@@ -537,14 +502,11 @@
         name="tables",
     )(fine_state, coarse_state)
 
-    answers, wants = pl.pallas_call(
+    answers = pl.pallas_call(
         reply_kernel,
-        out_shape=(
-            pltpu.HBM((line_size, SLOT_ROWS, LANES), f32),
-            pltpu.VMEM(tile, jnp.int32),
-        ),
-        in_specs=[vmem_spec()] * 4,
-        out_specs=(hbm_spec(), vmem_spec()),
+        out_shape=pltpu.HBM((line_size, SLOT_ROWS, LANES), f32),
+        in_specs=[vmem_spec()] * 2,
+        out_specs=hbm_spec(),
         scratch_shapes=[
             pltpu.SMEM((line_size, LANES), jnp.int32),
             pltpu.SemaphoreType.DMA,
@@ -552,19 +514,17 @@
         ],
         compiler_params=kernel_params(),
         name="answers",
-    )(near(codes), near(table), near(wants), near(other))
-    other = across(wants, 1)
+    )(near(codes), near(table))
     replies = exchange(answers)
 
-    partial, interior, wants = pl.pallas_call(
+    partial, interior = pl.pallas_call(
         functools.partial(interior_kernel, boxes),
         out_shape=(
             pltpu.HBM(fine_state.shape, f32),
             pltpu.HBM((boxes, COMPS, HALF, SMALL), f32),
-            pltpu.VMEM(tile, jnp.int32),
         ),
-        in_specs=[vmem_spec()] * 3,
-        out_specs=(hbm_spec(), hbm_spec(), vmem_spec()),
+        in_specs=[vmem_spec()],
+        out_specs=(hbm_spec(), hbm_spec()),
         scratch_shapes=[
             pltpu.VMEM(fine_state.shape, f32),
             pltpu.VMEM((boxes, COMPS, HALF, SMALL), f32),
@@ -573,44 +533,27 @@
         + [pltpu.VMEM((8, EDGE, LANES), f32), pltpu.SemaphoreType.DMA((2,))],
         compiler_params=kernel_params(),
         name="interior",
-    )(fine_state, near(wants), near(other))
-    other = across(wants, 2)
-
-
-    flux, sent = pl.pallas_call(
+    )(fine_state)
+
+
+    block = (COMPS, HALF, SMALL)
+    flux, *restricted = pl.pallas_call(
         functools.partial(flux_kernel, boxes, blocks, line_size),
-        out_shape=(
-            pltpu.VMEM((6 * boxes, SLOT_ROWS, LANES), f32),
-            pltpu.HBM((ring, COMPS, HALF, SMALL), f32),
-        ),
-        in_specs=[smem_spec()] * 2 + [hbm_spec()] + [vmem_spec()] * 4,
-        out_specs=(vmem_spec(), hbm_spec()),
-        scratch_shapes=[
-            pltpu.VMEM((boxes, COMPS, HALF, SMALL), f32),
-            pltpu.VMEM((boxes, COMPS, HALF, SMALL), f32),
-            pltpu.VMEM(tile, jnp.int32),
-            pltpu.SMEM(tile, jnp.int32),
-            pltpu.SemaphoreType.DMA((2,)),
-            pltpu.SemaphoreType.DMA((ring,)),
-        ],
+        out_shape=[pltpu.VMEM((6 * boxes, SLOT_ROWS, LANES), f32)]
+        + [pltpu.VMEM(block, f32)] * boxes,
+        in_specs=[smem_spec()] * 2 + [hbm_spec()] + [vmem_spec()] * 2,
+        out_specs=[vmem_spec()] * (1 + boxes),
+        scratch_shapes=[pltpu.VMEM((boxes,) + block, f32), pltpu.SemaphoreType.DMA],
         compiler_params=kernel_params(),
         name="fluxes",
-    )(
-        far(neighbours),
-        far(coarse_sources),
-        far(interior),
-        near(table),
-        near(replies),
-        near(wants),
-        near(other),
-    )
-    received = lax.all_to_all(sent, "gx", split_axis=0, concat_axis=0, tiled=True)
+    )(far(neighbours), far(coarse_sources), far(interior), near(table), near(replies))
 
     fine_next = pl.pallas_call(
         functools.partial(finish_kernel, boxes),
         out_shape=jax.ShapeDtypeStruct(fine_state.shape, f32),
         in_specs=[vmem_spec(), vmem_spec()],
-        out_specs=vmem_spec(),
+        out_specs=any_spec(),
+        scratch_shapes=[pltpu.VMEM(fine_state.shape, f32), pltpu.SemaphoreType.DMA((boxes,))],
         compiler_params=kernel_params(),
         name="finish",
     )(partial, near(flux))
@@ -624,16 +567,35 @@
         name="prior",
     )(coarse_state)
 
+    def shift(x, step):
+        return lax.ppermute(x, "gx", [(i, (i + step) % ring) for i in range(ring)])
+
+    gathered = {(0, b): restricted[b] for b in range(boxes)}
+    right, left = list(restricted), list(restricted)
+    half = ring // 2
+    for hop in range(1, half + 1):
+        for b in range(boxes):
+            if 2 * hop < ring or b % 2 == 0:
+                right[b] = shift(right[b], 1)
+                gathered[ring - hop, b] = right[b]
+            if 2 * hop < ring or b % 2 == 1:
+                left[b] = shift(left[b], -1)
+                gathered[hop, b] = left[b]
+
     coarse_next = pl.pallas_call(
-        functools.partial(place_kernel, boxes, line_size),
+        functools.partial(place_kernel, boxes, line_size, ring),
         out_shape=jax.ShapeDtypeStruct(coarse_state.shape, f32),
-        in_specs=[smem_spec(), any_spec(), vmem_spec()],
+        in_specs=[smem_spec(), any_spec()] + [vmem_spec()] * (boxes * ring),
         out_specs=any_spec(),
         scratch_shapes=[pltpu.SemaphoreType.DMA((blocks,))],
         input_output_aliases={1: 0},
         compiler_params=kernel_params(),
         name="place",
-    )(far(covering), prior, near(received))
+    )(
+        far(covering),
+        prior,
+        *[near(gathered[k, b]) for k in range(ring) for b in range(boxes)],
+    )
     return fine_next, coarse_next
 
 

time: 73.6 us -> 66.5 us (0.904)
  the two profiles are of different devices: /device:TPU:1 before, /device:TPU:2 now
where the time goes in v1:
time: 66.5 us; the launch traced here: 66.2 us
  starting transfers between devices  34.2 us (51%)
  Pallas kernels  20.2 us (30%)
  waiting for transfers between devices  11 us (17%)
  between operations  0.75 us (1%)
    ppermute x14, starting transfers between devices, shift(): return lax.ppermute(x, 'gx', [(i, (i + step) % ring) for i in range(ring)])  21.4 us
    all_to_all x2, starting transfers between devices, exchange(): return lax.all_to_all(x, PLANE, split_axis=0, concat_axis=0, tiled=True)  12.8 us
    all_to_all x2, waiting for transfers between devices, exchange(): return lax.all_to_all(x, PLANE, split_axis=0, concat_axis=0, tiled=True)  8.11 us
    pallas_call x1, Pallas kernels, body(): pl.pallas_call(functools.partial(interior_kernel, boxes), out_shape=(pltp...  5.86 us
    pallas_call x1, Pallas kernels, body(): pl.pallas_call(functools.partial(table_kernel, boxes, blocks), out_shape=...  3.88 us
    pallas_call x1, Pallas kernels, body(): pl.pallas_call(functools.partial(flux_kernel, boxes, blocks, line_size),...  3.23 us
    ppermute x14, waiting for transfers between devices, shift(): return lax.ppermute(x, 'gx', [(i, (i + step) % ring) for i in range(ring)])  2.88 us
    pallas_call x1, Pallas kernels, body(): pl.pallas_call(functools.partial(finish_kernel, boxes), out_shape=jax.Sha...  2.26 us
  transfers between devices with their start and end apart: 16, of which 7 were waited for; matrix products, arithmetic and copies ran while one was open for 0% of the time, Pallas kernels for 19%

profile of v1, /device:TPU:2, one launch (start us, length us, event | category | flops | bytes accessed | tf_op | source)
XLA Modules:
  0.0 66.2 jit_solution(13048518885035251223)
XLA Ops:
  0.6 1.4 %requests.1 = s32[32,128]{1,0:T(8,128)} custom-call(s32[2,6]{1,0:T(2,128)} %fine_ids.1, s32[2,6]{1,0:T(2,128)} %coarse_ids.1), custom_call_target="tpu_custom_call" | custom-call | tf_op jit(solution)/shard_map/requests/pallas_call | solution.py:488
  2.0 7.6 %all-to-all-start = ((s32[32,1,128]{2,1,0:T(1,128)}), s32[32,1,128]{2,1,0:T(1,128)S(1)}, u32[]{:S(2)}, u32[]{:S(2)}) async-start(s32[32,1,128]{2,1,0:T(1,128)} %bitcast.5), calls=%async_computation | async-start | bytes 32768 | tf_op jit(solution)/shard_map/all_to_all | solution.py:478
  9.6 3.9 %tables.1.table_ref = f32[60,40,128]{2,1,0:T(8,128)S(1)} custom-call(f32[2,5,32,1024]{3,2,1,0:T(8,128)} %fine_ref.4, f32[8,5,16,256]{3,2,1,0:T(8,128)} %x_ref.1), custom_call_target="tpu_custom_call" | custom-call | tf_op jit(solution)/shard_map/tables/pallas_call | solution.py:497
  13.5 2.2 %all-to-all-done = s32[32,1,128]{2,1,0:T(1,128)S(1)} async-done(((s32[32,1,128]{2,1,0:T(1,128)}), s32[32,1,128]{2,1,0:T(1,128)S(1)}, u32[]{:S(2)}, u32[]{:S(2)}) %all-to-all-start) | async-done | bytes 16416 | tf_op jit(solution)/shard_map/all_to_all | solution.py:478
  15.7 0.0 copy-start
  15.7 1.8 %answers.1 = f32[32,40,128]{2,1,0:T(8,128)} custom-call(s32[32,128]{1,0:T(8,128)S(1)} %bitcast.4, f32[60,40,128]{2,1,0:T(8,128)S(1)} %tables.1.table_ref), custom_call_target="tpu_custom_call" | custom-call | tf_op jit(solution)/shard_map/answers/pallas_call | solution.py:505
  17.5 5.2 %all-to-all-start.1 = ((f32[32,40,128]{2,1,0:T(8,128)}), f32[32,40,128]{2,1,0:T(8,128)S(1)}, u32[]{:S(2)}, u32[]{:S(2)}) async-start(f32[32,40,128]{2,1,0:T(8,128)} %answers.1), calls=%async_computation.1 | async-start | bytes 1310720 | tf_op jit(solution)/shard_map/all_to_all | solution.py:478
  22.7 0.0 copy-done
  22.8 5.9 %interior.1 = (f32[2,5,32,1024]{3,2,1,0:T(8,128)}, f32[2,5,16,256]{3,2,1,0:T(8,128)}) custom-call(f32[2,5,32,1024]{3,2,1,0:T(8,128)S(1)} %copy-done), custom_call_target="tpu_custom_call" | custom-call | tf_op jit(solution)/shard_map/interior/pallas_call | solution.py:520
  28.6 0.0 copy-start.1
  28.6 5.9 %all-to-all-done.1.replies_ref = f32[32,40,128]{2,1,0:T(8,128)S(1)} async-done(((f32[32,40,128]{2,1,0:T(8,128)}), f32[32,40,128]{2,1,0:T(8,128)S(1)}, u32[]{:S(2)}, u32[]{:S(2)}) %all-to-all-start.1) | async-done | bytes 655392 | tf_op jit(solution)/shard_map/all_to_all | solution.py:478
  34.5 0.0 copy-start.2
  34.5 3.2 %fluxes.1 = (f32[12,40,128]{2,1,0:T(8,128)S(1)}, f32[5,16,256]{2,1,0:T(8,128)S(1)}, f32[5,16,256]{2,1,0:T(8,128)S(1)}) custom-call(s32[2,6]{1,0:T(2,128)} %fine_ids.1, s32[2,6]{1,0:T(2,128)} %coarse_ids.1, f32[2,5,16,256]{3,2,1,0:T(8,128)} %get-tuple-element.8.restricted_ref, f32[60,40,128]{2,1,0:T(8,128)S(1)} %tables.1.table_ref, ...), custom_call_target="tpu_custom_call" | custom-call | tf_op jit(solution)/shard_map/fluxes/pallas_call | solution.py:540
  37.8 2.0 %collective-permute-start.6 = (f32[5,16,256]{2,1,0:T(8,128)S(1)}, f32[5,16,256]{2,1,0:T(8,128)S(1)}, u32[]{:S(2)}, u32[]{:S(2)}) collective-permute-start(f32[5,16,256]{2,1,0:T(8,128)S(1)} %get-tuple-element.10.rest_0_), channel_id=1, source_target_pairs={{0,32},{32,64},{64,96},{96,128},{128,160},{160,192},{192,224},{224... | collective-permute-start | bytes 245768 | tf_op jit(solution)/shard_map/ppermute | solution.py:571
  39.8 4.0 %collective-permute-start.1 = (f32[5,16,256]{2,1,0:T(8,128)S(1)}, f32[5,16,256]{2,1,0:T(8,128)S(1)}, u32[]{:S(2)}, u32[]{:S(2)}) collective-permute-start(f32[5,16,256]{2,1,0:T(8,128)S(1)} %get-tuple-element.11.rest_1_), channel_id=1, source_target_pairs={{0,224},{32,0},{64,32},{96,64},{128,96},{160,128},{192,160},{224,1... | collective-permute-start | bytes 245768 | tf_op jit(solution)/shard_map/ppermute | solution.py:571
  43.7 1.9 %collective-permute-start = (f32[5,16,256]{2,1,0:T(8,128)S(1)}, f32[5,16,256]{2,1,0:T(8,128)S(1)}, u32[]{:S(2)}, u32[]{:S(2)}) collective-permute-start(f32[5,16,256]{2,1,0:T(8,128)S(1)} %get-tuple-element.10.rest_0_), channel_id=1, source_target_pairs={{0,224},{32,0},{64,32},{96,64},{128,96},{160,128},{192,160},{224,1... | collective-permute-start | bytes 245768 | tf_op jit(solution)/shard_map/ppermute | solution.py:571
  45.7 0.1 collective-permute-start.11
  45.8 0.9 %collective-permute-done.6.rest_14_ = f32[5,16,256]{2,1,0:T(8,128)S(1)} collective-permute-done((f32[5,16,256]{2,1,0:T(8,128)S(1)}, f32[5,16,256]{2,1,0:T(8,128)S(1)}, u32[]{:S(2)}, u32[]{:S(2)}) %collective-permute-start.6) | collective-permute-done | bytes 81952 | tf_op jit(solution)/shard_map/ppermute | solution.py:571
  46.7 0.0 collective-permute-start.7
  46.7 0.0 collective-permute-done.1.rest_3_
  46.7 3.4 %collective-permute-start.3 = (f32[5,16,256]{2,1,0:T(8,128)S(1)}, f32[5,16,256]{2,1,0:T(8,128)S(1)}, u32[]{:S(2)}, u32[]{:S(2)}) collective-permute-start(f32[5,16,256]{2,1,0:T(8,128)S(1)} %collective-permute-done.1.rest_3_), channel_id=1, source_target_pairs={{0,224},{32,0},{64,32},{96,64},{128,96},{160,128},{192,160},{224,1... | collective-permute-start | bytes 245768 | tf_op jit(solution)/shard_map/ppermute | solution.py:571
  50.1 0.0 collective-permute-done.rest_2_
  50.1 1.4 %collective-permute-start.2 = (f32[5,16,256]{2,1,0:T(8,128)S(1)}, f32[5,16,256]{2,1,0:T(8,128)S(1)}, u32[]{:S(2)}, u32[]{:S(2)}) collective-permute-start(f32[5,16,256]{2,1,0:T(8,128)S(1)} %collective-permute-done.rest_2_), channel_id=1, source_target_pairs={{0,224},{32,0},{64,32},{96,64},{128,96},{160,128},{192,160},{224,1... | collective-permute-start | bytes 245768 | tf_op jit(solution)/shard_map/ppermute | solution.py:571
  51.5 0.6 collective-permute-done.11.rest_15_
  52.1 0.1 collective-permute-start.12
  52.1 0.8 %collective-permute-done.7.rest_12_ = f32[5,16,256]{2,1,0:T(8,128)S(1)} collective-permute-done((f32[5,16,256]{2,1,0:T(8,128)S(1)}, f32[5,16,256]{2,1,0:T(8,128)S(1)}, u32[]{:S(2)}, u32[]{:S(2)}) %collective-permute-start.7) | collective-permute-done | bytes 81952 | tf_op jit(solution)/shard_map/ppermute | solution.py:571
  53.0 0.0 collective-permute-start.8
  53.0 0.0 collective-permute-done.3.rest_5_
  53.0 3.5 %collective-permute-start.5 = (f32[5,16,256]{2,1,0:T(8,128)S(1)}, f32[5,16,256]{2,1,0:T(8,128)S(1)}, u32[]{:S(2)}, u32[]{:S(2)}) collective-permute-start(f32[5,16,256]{2,1,0:T(8,128)S(1)} %collective-permute-done.3.rest_5_), channel_id=1, source_target_pairs={{0,224},{32,0},{64,32},{96,64},{128,96},{160,128},{192,160},{224,1... | collective-permute-start | bytes 245768 | tf_op jit(solution)/shard_map/ppermute | solution.py:571
  56.4 0.0 collective-permute-done.2.rest_4_
  56.4 0.9 %collective-permute-start.4 = (f32[5,16,256]{2,1,0:T(8,128)S(1)}, f32[5,16,256]{2,1,0:T(8,128)S(1)}, u32[]{:S(2)}, u32[]{:S(2)}) collective-permute-start(f32[5,16,256]{2,1,0:T(8,128)S(1)} %collective-permute-done.2.rest_4_), channel_id=1, source_target_pairs={{0,224},{32,0},{64,32},{96,64},{128,96},{160,128},{192,160},{224,1... | collective-permute-start | bytes 245768 | tf_op jit(solution)/shard_map/ppermute | solution.py:571
  57.4 0.4 collective-permute-done.12.rest_13_
  57.7 0.7 %collective-permute-start.13 = (f32[5,16,256]{2,1,0:T(8,128)S(1)}, f32[5,16,256]{2,1,0:T(8,128)S(1)}, u32[]{:S(2)}, u32[]{:S(2)}) collective-permute-start(f32[5,16,256]{2,1,0:T(8,128)S(1)} %collective-permute-done.12.rest_13_), channel_id=1, source_target_pairs={{0,32},{32,64},{64,96},{96,128},{128,160},{160,192},{192,224},{224... | collective-permute-start | bytes 245768 | tf_op jit(solution)/shard_map/ppermute | solution.py:571
  58.4 0.2 collective-permute-done.8.rest_10_
  58.6 0.0 collective-permute-start.9
  58.6 0.0 collective-permute-done.5.rest_7_
  58.6 3.5 %collective-permute-start.10 = (f32[5,16,256]{2,1,0:T(8,128)S(1)}, f32[5,16,256]{2,1,0:T(8,128)S(1)}, u32[]{:S(2)}, u32[]{:S(2)}) collective-permute-start(f32[5,16,256]{2,1,0:T(8,128)S(1)} %collective-permute-done.5.rest_7_), channel_id=1, source_target_pairs={{0,224},{32,0},{64,32},{96,64},{128,96},{160,128},{192,160},{224,1... | collective-permute-start | bytes 245768 | tf_op jit(solution)/shard_map/ppermute | solution.py:571
  62.1 0.0 copy-done.1
  62.1 0.9 %prior.1._ = f32[8,5,16,256]{3,2,1,0:T(8,128)} custom-call(f32[8,5,16,256]{3,2,1,0:T(8,128)S(1)} %copy-done.1), custom_call_target="tpu_custom_call" | custom-call | tf_op jit(solution)/shard_map/prior/pallas_call | solution.py:561
  62.9 0.0 copy-done.2
  62.9 2.3 %finish.1 = f32[2,5,32,1024]{3,2,1,0:T(8,128)} custom-call(f32[2,5,32,1024]{3,2,1,0:T(8,128)S(1)} %copy-done.2, f32[12,40,128]{2,1,0:T(8,128)S(1)} %get-tuple-element.9.flux_ref), custom_call_target="tpu_custom_call" | custom-call | tf_op jit(solution)/shard_map/finish/pallas_call | solution.py:551
  65.2 0.0 collective-permute-done.4.rest_6_
  65.2 0.0 collective-permute-done.13.rest_11_
  65.2 0.0 collective-permute-done.9.rest_8_
  65.2 0.0 collective-permute-done.10.rest_9_
  65.3 0.9 %place.1 = f32[8,5,16,256]{3,2,1,0:T(8,128)} custom-call(s32[8]{0:T(128)} %covering_ref.1, f32[8,5,16,256]{3,2,1,0:T(8,128)} %prior.1._, f32[5,16,256]{2,1,0:T(8,128)S(1)} %get-tuple-element.10.rest_0_, f32[5,16,256]{2,1,0:T(8,128)S(1)} %get-tuple-element.11.rest_1_, f32[5,16,256]{2,1,0:T(8,128)S(1)} %collective-permute-done.rest_2_, ...), custom_call_target="tpu_custom_call", output_to_operand_aliasing={{}: (1, {})} | custom-call | tf_op jit(solution)/shard_map/place/pallas_call | solution.py:585
Async XLA Ops:
  2.0 13.7 %all-to-all-start = ((s32[32,1,128]{2,1,0:T(1,128)}), s32[32,1,128]{2,1,0:T(1,128)S(1)}, u32[]{:S(2)}, u32[]{:S(2)}) async-start(s32[32,1,128]{2,1,0:T(1,128)} %bitcast.5), calls=%async_computation | async-start | bytes 32768 | tf_op jit(solution)/shard_map/all_to_all | solution.py:478
  15.7 7.0 %copy-start = (f32[2,5,32,1024]{3,2,1,0:T(8,128)S(1)}, f32[2,5,32,1024]{3,2,1,0:T(8,128)}, u32[]{:S(2)}) copy-start(f32[2,5,32,1024]{3,2,1,0:T(8,128)} %fine_ref.4) | copy-start | bytes 3932164
  17.5 17.0 %all-to-all-start.1 = ((f32[32,40,128]{2,1,0:T(8,128)}), f32[32,40,128]{2,1,0:T(8,128)S(1)}, u32[]{:S(2)}, u32[]{:S(2)}) async-start(f32[32,40,128]{2,1,0:T(8,128)} %answers.1), calls=%async_computation.1 | async-start | bytes 1310720 | tf_op jit(solution)/shard_map/all_to_all | solution.py:478
  28.6 33.4 %copy-start.1 = (f32[8,5,16,256]{3,2,1,0:T(8,128)S(1)}, f32[8,5,16,256]{3,2,1,0:T(8,128)}, u32[]{:S(2)}) copy-start(f32[8,5,16,256]{3,2,1,0:T(8,128)} %x_ref.1) | copy-start | bytes 1966084
  34.5 28.4 %copy-start.2 = (f32[2,5,32,1024]{3,2,1,0:T(8,128)S(1)}, f32[2,5,32,1024]{3,2,1,0:T(8,128)}, u32[]{:S(2)}) copy-start(f32[2,5,32,1024]{3,2,1,0:T(8,128)} %get-tuple-element.7.partial_ref) | copy-start | bytes 3932164
  37.8 8.9 %collective-permute-start.6 = (f32[5,16,256]{2,1,0:T(8,128)S(1)}, f32[5,16,256]{2,1,0:T(8,128)S(1)}, u32[]{:S(2)}, u32[]{:S(2)}) collective-permute-start(f32[5,16,256]{2,1,0:T(8,128)S(1)} %get-tuple-element.10.rest_0_), channel_id=1, source_target_pairs={{0,32},{32,64},{64,96},{96,128},{128,160},{160,192},{192,224},{224... | collective-permute-start | bytes 245768 | tf_op jit(solution)/shard_map/ppermute | solution.py:571
  39.8 6.9 %collective-permute-start.1 = (f32[5,16,256]{2,1,0:T(8,128)S(1)}, f32[5,16,256]{2,1,0:T(8,128)S(1)}, u32[]{:S(2)}, u32[]{:S(2)}) collective-permute-start(f32[5,16,256]{2,1,0:T(8,128)S(1)} %get-tuple-element.11.rest_1_), channel_id=1, source_target_pairs={{0,224},{32,0},{64,32},{96,64},{128,96},{160,128},{192,160},{224,1... | collective-permute-start | bytes 245768 | tf_op jit(solution)/shard_map/ppermute | solution.py:571
  43.7 6.4 %collective-permute-start = (f32[5,16,256]{2,1,0:T(8,128)S(1)}, f32[5,16,256]{2,1,0:T(8,128)S(1)}, u32[]{:S(2)}, u32[]{:S(2)}) collective-permute-start(f32[5,16,256]{2,1,0:T(8,128)S(1)} %get-tuple-element.10.rest_0_), channel_id=1, source_target_pairs={{0,224},{32,0},{64,32},{96,64},{128,96},{160,128},{192,160},{224,1... | collective-permute-start | bytes 245768 | tf_op jit(solution)/shard_map/ppermute | solution.py:571
  45.7 6.4 %collective-permute-start.11 = (f32[5,16,256]{2,1,0:T(8,128)S(1)}, f32[5,16,256]{2,1,0:T(8,128)S(1)}, u32[]{:S(2)}, u32[]{:S(2)}) collective-permute-start(f32[5,16,256]{2,1,0:T(8,128)S(1)} %get-tuple-element.11.rest_1_), channel_id=1, source_target_pairs={{0,32},{32,64},{64,96},{96,128},{128,160},{160,192},{192,224},{224... | collective-permute-start | bytes 245768 | tf_op jit(solution)/shard_map/ppermute | solution.py:571
  46.7 6.3 %collective-permute-start.7 = (f32[5,16,256]{2,1,0:T(8,128)S(1)}, f32[5,16,256]{2,1,0:T(8,128)S(1)}, u32[]{:S(2)}, u32[]{:S(2)}) collective-permute-start(f32[5,16,256]{2,1,0:T(8,128)S(1)} %collective-permute-done.6.rest_14_), channel_id=1, source_target_pairs={{0,32},{32,64},{64,96},{96,128},{128,160},{160,192},{192,224},{224... | collective-permute-start | bytes 245768 | tf_op jit(solution)/shard_map/ppermute | solution.py:571
  46.7 6.3 %collective-permute-start.3 = (f32[5,16,256]{2,1,0:T(8,128)S(1)}, f32[5,16,256]{2,1,0:T(8,128)S(1)}, u32[]{:S(2)}, u32[]{:S(2)}) collective-permute-start(f32[5,16,256]{2,1,0:T(8,128)S(1)} %collective-permute-done.1.rest_3_), channel_id=1, source_target_pairs={{0,224},{32,0},{64,32},{96,64},{128,96},{160,128},{192,160},{224,1... | collective-permute-start | bytes 245768 | tf_op jit(solution)/shard_map/ppermute | solution.py:571
  50.1 6.3 %collective-permute-start.2 = (f32[5,16,256]{2,1,0:T(8,128)S(1)}, f32[5,16,256]{2,1,0:T(8,128)S(1)}, u32[]{:S(2)}, u32[]{:S(2)}) collective-permute-start(f32[5,16,256]{2,1,0:T(8,128)S(1)} %collective-permute-done.rest_2_), channel_id=1, source_target_pairs={{0,224},{32,0},{64,32},{96,64},{128,96},{160,128},{192,160},{224,1... | collective-permute-start | bytes 245768 | tf_op jit(solution)/shard_map/ppermute | solution.py:571
  52.1 5.7 %collective-permute-start.12 = (f32[5,16,256]{2,1,0:T(8,128)S(1)}, f32[5,16,256]{2,1,0:T(8,128)S(1)}, u32[]{:S(2)}, u32[]{:S(2)}) collective-permute-start(f32[5,16,256]{2,1,0:T(8,128)S(1)} %collective-permute-done.11.rest_15_), channel_id=1, source_target_pairs={{0,32},{32,64},{64,96},{96,128},{128,160},{160,192},{192,224},{224... | collective-permute-start | bytes 245768 | tf_op jit(solution)/shard_map/ppermute | solution.py:571
  53.0 5.7 %collective-permute-start.8 = (f32[5,16,256]{2,1,0:T(8,128)S(1)}, f32[5,16,256]{2,1,0:T(8,128)S(1)}, u32[]{:S(2)}, u32[]{:S(2)}) collective-permute-start(f32[5,16,256]{2,1,0:T(8,128)S(1)} %collective-permute-done.7.rest_12_), channel_id=1, source_target_pairs={{0,32},{32,64},{64,96},{96,128},{128,160},{160,192},{192,224},{224... | collective-permute-start | bytes 245768 | tf_op jit(solution)/shard_map/ppermute | solution.py:571
  53.0 5.7 %collective-permute-start.5 = (f32[5,16,256]{2,1,0:T(8,128)S(1)}, f32[5,16,256]{2,1,0:T(8,128)S(1)}, u32[]{:S(2)}, u32[]{:S(2)}) collective-permute-start(f32[5,16,256]{2,1,0:T(8,128)S(1)} %collective-permute-done.3.rest_5_), channel_id=1, source_target_pairs={{0,224},{32,0},{64,32},{96,64},{128,96},{160,128},{192,160},{224,1... | collective-permute-start | bytes 245768 | tf_op jit(solution)/shard_map/ppermute | solution.py:571
  56.4 8.8 %collective-permute-start.4 = (f32[5,16,256]{2,1,0:T(8,128)S(1)}, f32[5,16,256]{2,1,0:T(8,128)S(1)}, u32[]{:S(2)}, u32[]{:S(2)}) collective-permute-start(f32[5,16,256]{2,1,0:T(8,128)S(1)} %collective-permute-done.2.rest_4_), channel_id=1, source_target_pairs={{0,224},{32,0},{64,32},{96,64},{128,96},{160,128},{192,160},{224,1... | collective-permute-start | bytes 245768 | tf_op jit(solution)/shard_map/ppermute | solution.py:571
  57.7 7.5 %collective-permute-start.13 = (f32[5,16,256]{2,1,0:T(8,128)S(1)}, f32[5,16,256]{2,1,0:T(8,128)S(1)}, u32[]{:S(2)}, u32[]{:S(2)}) collective-permute-start(f32[5,16,256]{2,1,0:T(8,128)S(1)} %collective-permute-done.12.rest_13_), channel_id=1, source_target_pairs={{0,32},{32,64},{64,96},{96,128},{128,160},{160,192},{192,224},{224... | collective-permute-start | bytes 245768 | tf_op jit(solution)/shard_map/ppermute | solution.py:571
  58.6 6.6 %collective-permute-start.9 = (f32[5,16,256]{2,1,0:T(8,128)S(1)}, f32[5,16,256]{2,1,0:T(8,128)S(1)}, u32[]{:S(2)}, u32[]{:S(2)}) collective-permute-start(f32[5,16,256]{2,1,0:T(8,128)S(1)} %collective-permute-done.8.rest_10_), channel_id=1, source_target_pairs={{0,32},{32,64},{64,96},{96,128},{128,160},{160,192},{192,224},{224... | collective-permute-start | bytes 245768 | tf_op jit(solution)/shard_map/ppermute | solution.py:571
  58.6 6.6 %collective-permute-start.10 = (f32[5,16,256]{2,1,0:T(8,128)S(1)}, f32[5,16,256]{2,1,0:T(8,128)S(1)}, u32[]{:S(2)}, u32[]{:S(2)}) collective-permute-start(f32[5,16,256]{2,1,0:T(8,128)S(1)} %collective-permute-done.5.rest_7_), channel_id=1, source_target_pairs={{0,224},{32,0},{64,32},{96,64},{128,96},{160,128},{192,160},{224,1... | collective-permute-start | bytes 245768 | tf_op jit(solution)/shard_map/ppermute | solution.py:571
